TPU v7x, 512 devices: a whole 4x4x16 slice. The times are simulated.
512 devices in a mesh: expert: 64 (over x, z), dp: 4 (over y), test: 2 (over core).
Axes of the slice: x: 4, y: 4, z: 16, core: 2. Of those that a mesh axis runs over, the one named last changes fastest.
Arguments:
- tokens: bfloat16 [16384, 3584], P(('expert', 'dp'), 'test'), may hold values from -6 to 6
- out_grad: bfloat16 [16384, 3584], P(('expert', 'dp'), 'test'), may hold values from -6 to 6
- route_ids: int32 [16384, 8], P(('expert', 'dp')), may hold values from 0 to 255, as said below
- route_slots: int32 [16384, 8], P(('expert', 'dp')), may hold values from -1 to 1, as said below
- route_weight: bfloat16 [16384, 8], P(('expert', 'dp')), may hold values from 0.19921875 to 1
- w_gate: bfloat16 [64, 3584, 1024], P('expert', None, ('dp', 'test')), may hold values from -0.09375 to 0.09375
- w_up: bfloat16 [64, 3584, 1024], P('expert', None, ('dp', 'test')), may hold values from -0.09375 to 0.09375
- w_down: bfloat16 [64, 1024, 3584], P('expert', ('dp', 'test')), may hold values from -0.1875 to 0.1875
- proj_hidden: bfloat16 [64, 64, 1024], P('expert', None, ('dp', 'test')), may hold values from -0.1875 to 0.1875
- proj_grad: bfloat16 [64, 64, 3584], P('expert'), may hold values from -0.09375 to 0.09375
- test_feats: bfloat16 [64, 256, 4096], P('expert', 'test'), may hold values from -0.09375 to 0.09375
Outputs:
- in_grad: bfloat16 [16384, 3584], P(('expert', 'dp'), 'test')
- scores: float32 [16384, 256], P(('expert', 'dp'), 'test')
Inputs may be any that keep to these rules, and one draw needn't show every extreme that they name: `route_ids`: each row names 8 different experts. `route_slots`: A route's slot is -1 exactly when its expert is 64 or more, or when 2 earlier tokens of the same aligned block of 64 rows already take that expert; otherwise it is the number of earlier tokens of that block routed to that expert.
All inputs are finite; a program needn't handle non-finite values.
Results may differ from a plain program's by a relative error of at most 0.0065.
Values may be sent and summed in bfloat16 or wider, within the bound.
A program may use at most 64 MiB of HBM per device.

v0:
```python
import jax
import jax.numpy as jnp
from jax import lax
from jax.sharding import PartitionSpec as P

CAP = 2


def pick_tables(ids_in, slots_in, weights_in, experts):
    live_mask = (slots_in >= 0) & (ids_in < experts)
    slot_code = jnp.where(live_mask, ids_in * CAP + slots_in, -1)
    columns = jnp.arange(experts * CAP, dtype=jnp.int32)
    matches = slot_code[:, :, None] == columns[None, None, :]
    picks = jnp.sum(matches.astype(jnp.float32), axis=1)
    weighted = jnp.sum(jnp.where(matches, weights_in.astype(jnp.float32)[:, :, None], 0.0), axis=1)
    return (picks.astype(jnp.bfloat16), weighted.astype(jnp.bfloat16))


def dot(a, b, ca, cb):
    return lax.dot_general(a, b, (((ca,), (cb,)), ((), ())), preferred_element_type=jnp.float32)


def on_device(
    tokens,
    out_grad,
    route_ids,
    route_slots,
    route_weight,
    w_gate,
    w_up,
    w_down,
    proj_hidden,
    proj_grad,
    test_feats,
):
    experts = lax.axis_size("expert")
    groups = lax.axis_size("dp")
    halves = lax.axis_size("test")
    half = tokens.shape[1]
    slots = experts * CAP
    pick, weighted = pick_tables(route_ids, route_slots, route_weight, experts)
    in_buf = dot(pick, tokens, 0, 0).astype(jnp.bfloat16)
    grad_buf = dot(weighted, out_grad, 0, 0).astype(jnp.bfloat16)

    def exchange(rows):
        width = rows.shape[1]
        moved = lax.all_to_all(
            rows.reshape(experts, CAP, width), "expert", split_axis=0, concat_axis=0, tiled=True
        )
        return moved.reshape(slots, width)

    def spread(rows):
        full = lax.all_gather(rows, ("dp", "test"), axis=0, tiled=True)
        full = full.reshape(groups, halves, slots, half)
        return [full[:, h].reshape(groups * slots, half) for h in range(halves)]

    mine_in = exchange(in_buf)
    ins = spread(mine_in)
    mine_grad = exchange(grad_buf)
    grads = spread(mine_grad)
    gate_w, up_w, down_w = (w_gate[0], w_up[0], w_down[0])

    def cut(arr, h, axis):
        return lax.slice_in_dim(arr, h * half, (h + 1) * half, axis=axis)

    gate_pre = sum((dot(ins[h], cut(gate_w, h, 0), 1, 0) for h in range(halves)))
    up_pre = sum((dot(ins[h], cut(up_w, h, 0), 1, 0) for h in range(halves)))
    sig = jax.nn.sigmoid(gate_pre)
    act = gate_pre * sig
    hidden = (act * up_pre).astype(jnp.bfloat16)
    proj_part = dot(hidden, proj_hidden[0], 1, 1)
    hid_grad = sum((dot(grads[h], cut(down_w, h, 1), 1, 1) for h in range(halves)))
    up_grad = (hid_grad * act).astype(jnp.bfloat16)
    gate_grad = (hid_grad * up_pre * sig * (1.0 + gate_pre * (1.0 - sig))).astype(jnp.bfloat16)
    parts = [
        (dot(gate_grad, cut(gate_w, h, 0), 1, 1) + dot(up_grad, cut(up_w, h, 0), 1, 1)).astype(
            jnp.bfloat16
        )
        for h in range(halves)
    ]
    parts = jnp.stack([p.reshape(groups, slots, half) for p in parts], axis=1)
    mine_back = lax.psum_scatter(
        parts.reshape(groups * halves * slots, half),
        ("dp", "test"),
        scatter_dimension=0,
        tiled=True,
    )
    back = exchange(mine_back.astype(jnp.bfloat16))
    in_grad = dot(pick, back, 1, 0).astype(jnp.bfloat16)
    hidden_vec = lax.psum(proj_part, ("dp", "test"))
    me = lax.axis_index("dp")
    hid_mine = lax.dynamic_slice_in_dim(hidden_vec, me * slots, slots, 0)
    grad_mine = sum(
        (
            dot(
                lax.dynamic_slice_in_dim(grads[h], me * slots, slots, 0),
                cut(proj_grad[0], h, 1),
                1,
                1,
            )
            for h in range(halves)
        )
    )
    feature = (hid_mine[:, :, None] * grad_mine[:, None, :]).reshape(slots, -1).astype(jnp.bfloat16)
    score = dot(feature, test_feats[0], 1, 1).astype(jnp.bfloat16)
    scores = dot(pick, exchange(score), 1, 0)
    return (in_grad, scores)


def solution(mesh):
    placed = (
        P(("expert", "dp"), "test"),
        P(("expert", "dp"), "test"),
        P(("expert", "dp"), None),
        P(("expert", "dp"), None),
        P(("expert", "dp"), None),
        P("expert", None, ("dp", "test")),
        P("expert", None, ("dp", "test")),
        P("expert", ("dp", "test"), None),
        P("expert", None, ("dp", "test")),
        P("expert", None, None),
        P("expert", "test", None),
    )
    return jax.shard_map(
        on_device,
        mesh=mesh,
        in_specs=placed,
        out_specs=(P(("expert", "dp"), "test"), P(("expert", "dp"), "test")),
        check_vma=False,
    )
```

profile of v0, /device:TPU:31, one launch (start us, length us, event | category | flops | bytes accessed | tf_op | source)
XLA Modules:
  0.0 316.4 jit_solution(14806735404021677156)
XLA Ops:
  7.2 0.8 add_select_fusion
  8.0 0.1 copy.21
  8.1 0.8 copy.22
  8.9 0.2 select_reduce_fusion
  9.1 1.3 convolution_convert_fusion.1
  10.4 0.2 reshape.58
  10.6 45.3 %all_to_all.20 = bf16[64,2,1792]{2,1,0:T(2,128)(2,1)S(1)} all-to-all(bf16[64,2,1792]{2,1,0:T(2,128)(2,1)S(1)} %reshape.58), channel_id=1, replica_groups=mesh['expert'=64,'dp'=4,'test'=2] {'expert'}, dimensions={0} | all-to-all | bytes 917504 | tf_op jit(solution)/shard_map/all_to_all | solution.py:47
  55.9 1.0 reshape.59
  56.9 0.3 convolution_convert_fusion
  57.2 0.2 reshape.61
  57.4 34.0 %all_to_all.21 = bf16[64,2,1792]{2,1,0:T(2,128)(2,1)S(1)} all-to-all(bf16[64,2,1792]{2,1,0:T(2,128)(2,1)S(1)} %reshape.61), channel_id=1, replica_groups=mesh['expert'=64,'dp'=4,'test'=2] {'expert'}, dimensions={0} | all-to-all | bytes 917504 | tf_op jit(solution)/shard_map/all_to_all | solution.py:47
  91.4 0.9 reshape.62
  92.4 0.0 all-reduce.2.cloned.1.call-start
  92.4 3.6 %fusion.41 = (bf16[4,1,128,1792]{3,2,1,0:T(8,128)(2,1)}, bf16[4,1,128,1792]{3,2,1,0:T(8,128)(2,1)S(1)}) fusion(bf16[4,2,128,1792]{3,2,1,0:T(8,128)(2,1)} %bitcast.73), kind=kLoop, calls=%fused_computation.61 | loop fusion | bytes 7340032 | tf_op jit(solution)/shard_map/slice | solution.py:55
  96.0 31.3 %all-gather.5.cloned.1.call-done = bf16[1024,1792]{1,0:T(8,128)(2,1)} async-done(((bf16[128,1792]{1,0:T(8,128)(2,1)}), bf16[1024,1792]{1,0:T(8,128)(2,1)}) %all-gather.5.cloned.1.call-update) | async-done | bytes 3670032 | tf_op jit(solution)/shard_map/all_gather | solution.py:53
  127.4 2.4 fusion.42
  129.8 0.6 fusion.9
  130.4 0.5 copy-done.3
  130.9 0.6 fusion.14
  131.6 0.6 convolution_add_fusion.1
  132.3 0.6 convolution_add_fusion
  132.9 0.5 copy-done.7
  133.4 0.6 fusion.2
  134.1 0.4 copy-done.5
  134.5 0.6 multiply_convert_fusion.2
  135.1 2.4 fusion.4
  137.6 2.5 fusion.7
  140.1 0.9 fusion.30
  141.0 3.0 add_convert_fusion
  144.0 0.3 copy-done.1
  144.3 0.2 copy-done.4
  144.5 0.6 add_convert_fusion.1
  145.2 2.1 pad_maximum_fusion
  147.3 1.0 copy-done.6
  148.3 0.3 fusion.17
  148.6 1.3 convolution_add_fusion.3
  149.9 66.4 %all-reduce.2.cloned.1.call-done = f32[512,64]{0,1:T(8,128)} async-done(((f32[512,64]{0,1:T(8,128)}), f32[512,64]{0,1:T(8,128)}) %all-reduce.2.cloned.1.call-update) | async-done | bytes 131088 | tf_op jit(solution)/shard_map/psum | solution.py:90
  216.3 0.8 constant_dynamic-slice_fusion
  217.1 0.3 multiply_convert_fusion
  217.4 1.1 convolution_convert_fusion.3
  218.5 15.3 %all-to-all-start.3 = ((bf16[64,2,128]{2,1,0:T(2,128)(2,1)}), bf16[64,2,128]{2,1,0:T(2,128)(2,1)S(1)}, u32[]{:S(2)}, u32[]{:S(2)}) async-start(bf16[64,2,128]{2,1,0:T(2,128)(2,1)} %bitcast.20), calls=%async_computation.4 | async-start | bytes 65536 | tf_op jit(solution)/shard_map/all_to_all | solution.py:47
  233.8 29.1 %reduce-scatter.2.cloned.1.call-done = bf16[128,1792]{1,0:T(8,128)(2,1)} async-done(((bf16[1024,1792]{1,0:T(8,128)(2,1)}), bf16[128,1792]{1,0:T(8,128)(2,1)}) %reduce-scatter.2.cloned.1.call-update) | async-done | bytes 458768 | tf_op jit(solution)/shard_map/reduce_scatter | solution.py:82
  262.9 2.0 reshape.65
  264.9 15.0 %all-to-all-start.2 = ((bf16[64,2,1792]{2,1,0:T(2,128)(2,1)}), bf16[64,2,1792]{2,1,0:T(2,128)(2,1)S(1)}, u32[]{:S(2)}, u32[]{:S(2)}) async-start(bf16[64,2,1792]{2,1,0:T(2,128)(2,1)} %reshape.65), calls=%async_computation.3 | async-start | bytes 917504 | tf_op jit(solution)/shard_map/all_to_all | solution.py:47
  279.9 0.7 fusion.43
  280.6 28.2 %all-to-all-done.2 = bf16[64,2,1792]{2,1,0:T(2,128)(2,1)S(1)} async-done(((bf16[64,2,1792]{2,1,0:T(2,128)(2,1)}), bf16[64,2,1792]{2,1,0:T(2,128)(2,1)S(1)}, u32[]{:S(2)}, u32[]{:S(2)}) %all-to-all-start.2) | async-done | bytes 458784 | tf_op jit(solution)/shard_map/all_to_all | solution.py:47
  308.8 0.2 reshape.66
  309.0 0.9 convolution_convert_fusion.2
  (23 shorter events, 0.2 us)
Async XLA Ops:
  7.2 210.2 %copy-start = (bf16[1,128,4096]{2,1,0:T(8,128)(2,1)S(1)}, bf16[1,128,4096]{2,1,0:T(8,128)(2,1)}, u32[]{:S(2)}) copy-start(bf16[1,128,4096]{2,1,0:T(8,128)(2,1)} %param.21) | copy-start | bytes 3145732
  7.2 85.2 %all-gather.3.cloned.1.call-start = ((), (), s32[]{:S(2)}) async-start(), calls=%async_computation.5 | async-start | bytes 4128768 | tf_op jit(solution)/shard_map/all_gather | solution.py:53
  9.1 47.8 %copy-start.8 = (bf16[64,1792]{1,0:T(8,128)(2,1)S(1)}, bf16[64,1792]{1,0:T(8,128)(2,1)}, u32[]{:S(2)}) copy-start(bf16[64,1792]{1,0:T(8,128)(2,1)} %param.11) | copy-start | bytes 688132
  56.9 70.5 %all-gather.5.cloned.1.call-start = ((), (), s32[]{:S(2)}) async-start(), calls=%async_computation.6 | async-start | bytes 4128768 | tf_op jit(solution)/shard_map/all_gather | solution.py:53
  92.4 124.0 %all-reduce.2.cloned.1.call-start = ((), (), s32[]{:S(2)}) async-start(), calls=%async_computation.8 | async-start | bytes 262144 | tf_op jit(solution)/shard_map/psum | solution.py:90
  127.4 2.4 copy-start.2
  129.8 1.2 copy-start.3
  132.2 1.2 copy-start.7
  132.9 1.6 copy-start.5
  137.6 2.5 copy-start.9
  140.9 122.0 %reduce-scatter.2.cloned.1.call-start = ((), (), s32[]{:S(2)}) async-start(), calls=%async_computation.7 | async-start | bytes 4128768 | tf_op jit(solution)/shard_map/reduce_scatter | solution.py:82
  141.0 3.3 %copy-start.1 = (f32[512,1792]{1,0:T(8,128)S(1)}, f32[512,1792]{1,0:T(8,128)}, u32[]{:S(2)}) copy-start(f32[512,1792]{1,0:T(8,128)} %fusion.7) | copy-start | bytes 11010052
  141.0 3.5 %copy-start.4 = (bf16[1,3584,128]{2,1,0:T(8,128)(2,1)S(1)}, bf16[1,3584,128]{2,1,0:T(8,128)(2,1)}, u32[]{:S(2)}) copy-start(bf16[1,3584,128]{2,1,0:T(8,128)(2,1)} %param.17) | copy-start | bytes 2752516
  147.3 1.0 copy-start.6
  218.5 46.4 %all-to-all-start.3 = ((bf16[64,2,128]{2,1,0:T(2,128)(2,1)}), bf16[64,2,128]{2,1,0:T(2,128)(2,1)S(1)}, u32[]{:S(2)}, u32[]{:S(2)}) async-start(bf16[64,2,128]{2,1,0:T(2,128)(2,1)} %bitcast.20), calls=%async_computation.4 | async-start | bytes 65536 | tf_op jit(solution)/shard_map/all_to_all | solution.py:47
  264.9 43.9 %all-to-all-start.2 = ((bf16[64,2,1792]{2,1,0:T(2,128)(2,1)}), bf16[64,2,1792]{2,1,0:T(2,128)(2,1)S(1)}, u32[]{:S(2)}, u32[]{:S(2)}) async-start(bf16[64,2,1792]{2,1,0:T(2,128)(2,1)} %reshape.65), calls=%async_computation.3 | async-start | bytes 917504 | tf_op jit(solution)/shard_map/all_to_all | solution.py:47
Sparse Core Ops, SparseCore 0:
  57.0 30.6 all-gather.2
  92.5 34.8 all-gather.4
  141.1 75.2 all-reduce.1
  219.0 43.8 reduce-scatter.1
where the time goes:
time: 317 us; the launch traced here: 316 us
  waiting for transfers between devices  155 us (49%)
  blocking collectives  79.3 us (25%)
  starting transfers between devices  30.5 us (10%)
  matrix products  19.2 us (6%)
  local copies, waits for them, and re-layouts  15 us (5%)
  between operations  14 us (4%)
  other arithmetic  3.41 us (1%)
    all_to_all x2, blocking collectives, exchange(): lax.all_to_all(rows.reshape(experts, CAP, width), 'expert', split_axis=0,...  79.3 us
    psum x1, waiting for transfers between devices, on_device(): hidden_vec = lax.psum(proj_part, ('dp', 'test'))  66.4 us
    all_gather x2, waiting for transfers between devices, spread(): full = lax.all_gather(rows, ('dp', 'test'), axis=0, tiled=True)  31.3 us
    all_to_all x2, starting transfers between devices, exchange(): lax.all_to_all(rows.reshape(experts, CAP, width), 'expert', split_axis=0,...  30.3 us
    reduce_scatter x1, waiting for transfers between devices, on_device(): lax.psum_scatter(parts.reshape(groups * halves * slots, half), ('dp', 'te...  29.1 us
    all_to_all x2, waiting for transfers between devices, exchange(): lax.all_to_all(rows.reshape(experts, CAP, width), 'expert', split_axis=0,...  28.2 us
    dot_general x18, matrix products, dot(): lax.dot_general(a, b, (((ca,), (cb,)), ((), ())), preferred_element_type=...  19.2 us
  transfers between devices with their start and end apart: 6, of which 4 were waited for; matrix products, arithmetic and copies ran while one was open for 5% of the time, Pallas kernels for 0%

commit v1 on v0

--- a/solution.py
+++ b/solution.py
@@ -87,7 +87,7 @@
     )
     back = exchange(mine_back.astype(jnp.bfloat16))
     in_grad = dot(pick, back, 1, 0).astype(jnp.bfloat16)
-    hidden_vec = lax.psum(proj_part, ("dp", "test"))
+    hidden_vec = jnp.sum(lax.all_gather(proj_part, ("dp", "test")), axis=0)
     me = lax.axis_index("dp")
     hid_mine = lax.dynamic_slice_in_dim(hidden_vec, me * slots, slots, 0)
     grad_mine = sum(

time: 317 us -> 267 us (0.84)
  waiting for transfers between devices: 155 us -> 108 us
  matrix products: 19.2 us -> 15.5 us
    psum x1 -> x0, waiting for transfers between devices: 66.4 us -> none  [on_device(): hidden_vec = lax.psum(proj_part, ('dp', 'test'))]
    all_gather x0 -> x1, waiting for transfers between devices: none -> 19.6 us  [on_device(): hidden_vec = jnp.sum(lax.all_gather(proj_part, ('dp', 'test')), axis=0)]
    dot_general x18, matrix products: 19.2 us -> 15.5 us  [dot(): lax.dot_general(a, b, (((ca,), (cb,)), ((), ())), preferred_element_type=...]
  transfers between devices with their start and end apart: 6 -> 6, of which waited for: 4 -> 4; matrix products, arithmetic and copies ran while one was open for 5% -> 8% of each run, Pallas kernels for 0% -> 0%
where the time goes in v1:
time: 267 us; the launch traced here: 266 us
  waiting for transfers between devices  108 us (40%)
  blocking collectives  79.3 us (30%)
  starting transfers between devices  30.5 us (11%)
  local copies, waits for them, and re-layouts  15.8 us (6%)
  matrix products  15.5 us (6%)
  between operations  14 us (5%)
  other arithmetic  3.66 us (1%)
    all_to_all x2, blocking collectives, exchange(): lax.all_to_all(rows.reshape(experts, CAP, width), 'expert', split_axis=0,...  79.3 us
    all_gather x2, waiting for transfers between devices, spread(): full = lax.all_gather(rows, ('dp', 'test'), axis=0, tiled=True)  31.4 us
    all_to_all x2, starting transfers between devices, exchange(): lax.all_to_all(rows.reshape(experts, CAP, width), 'expert', split_axis=0,...  30.3 us
    reduce_scatter x1, waiting for transfers between devices, on_device(): lax.psum_scatter(parts.reshape(groups * halves * slots, half), ('dp', 'te...  28.5 us
    all_to_all x2, waiting for transfers between devices, exchange(): lax.all_to_all(rows.reshape(experts, CAP, width), 'expert', split_axis=0,...  28.2 us
    all_gather x1, waiting for transfers between devices, on_device(): hidden_vec = jnp.sum(lax.all_gather(proj_part, ('dp', 'test')), axis=0)  19.6 us
    dot_general x18, matrix products, dot(): lax.dot_general(a, b, (((ca,), (cb,)), ((), ())), preferred_element_type=...  15.5 us
    slice x2, local copies, waits for them, and re-layouts, spread(): return [full[:, h].reshape(groups * slots, half) for h in range(halves)]  6 us
  transfers between devices with their start and end apart: 6, of which 4 were waited for; matrix products, arithmetic and copies ran while one was open for 8% of the time, Pallas kernels for 0%

profile of v1, /device:TPU:31, one launch (start us, length us, event | category | flops | bytes accessed | tf_op | source)
XLA Modules:
  0.0 266.4 jit_solution(6131072850505431678)
XLA Ops:
  7.2 0.8 add_select_fusion
  8.0 0.1 copy.20
  8.1 0.8 copy.21
  8.9 0.2 select_reduce_fusion
  9.1 1.3 convolution_convert_fusion.1
  10.4 0.2 reshape.58
  10.6 45.3 %all_to_all.20 = bf16[64,2,1792]{2,1,0:T(2,128)(2,1)S(1)} all-to-all(bf16[64,2,1792]{2,1,0:T(2,128)(2,1)S(1)} %reshape.58), channel_id=1, replica_groups=mesh['expert'=64,'dp'=4,'test'=2] {'expert'}, dimensions={0} | all-to-all | bytes 917504 | tf_op jit(solution)/shard_map/all_to_all | solution.py:47
  55.9 0.9 reshape.59
  56.8 0.0 all-gather.7.cloned.1.call-start
  56.9 0.3 convolution_convert_fusion
  57.2 0.2 reshape.61
  57.4 34.0 %all_to_all.21 = bf16[64,2,1792]{2,1,0:T(2,128)(2,1)S(1)} all-to-all(bf16[64,2,1792]{2,1,0:T(2,128)(2,1)S(1)} %reshape.61), channel_id=1, replica_groups=mesh['expert'=64,'dp'=4,'test'=2] {'expert'}, dimensions={0} | all-to-all | bytes 917504 | tf_op jit(solution)/shard_map/all_to_all | solution.py:47
  91.4 0.9 reshape.62
  92.4 3.6 %fusion.41 = (bf16[4,1,128,1792]{3,2,1,0:T(8,128)(2,1)}, bf16[4,1,128,1792]{3,2,1,0:T(8,128)(2,1)S(1)}) fusion(bf16[4,2,128,1792]{3,2,1,0:T(8,128)(2,1)} %bitcast.78), kind=kLoop, calls=%fused_computation.62 | loop fusion | bytes 7340032 | tf_op jit(solution)/shard_map/slice | solution.py:55
  96.0 31.3 %all-gather.7.cloned.1.call-done = bf16[1024,1792]{1,0:T(8,128)(2,1)} async-done(((bf16[128,1792]{1,0:T(8,128)(2,1)}), bf16[1024,1792]{1,0:T(8,128)(2,1)}) %all-gather.7.cloned.1.call-update) | async-done | bytes 3670032 | tf_op jit(solution)/shard_map/all_gather | solution.py:53
  127.4 2.4 fusion.42
  129.8 0.6 fusion.9
  130.4 0.5 copy-done.3
  130.9 0.6 fusion.14
  131.6 0.6 convolution_add_fusion.1
  132.2 0.6 convolution_add_fusion
  132.9 0.7 copy-done.7
  133.6 0.9 fusion.30
  134.5 0.0 reduce-scatter.2.cloned.1.call-start
  134.6 1.8 fusion.2
  136.4 1.7 multiply_convert_fusion.2
  138.2 0.6 fusion.4
  138.8 0.6 fusion.7
  139.5 0.5 copy-done.4
  140.0 0.6 add_convert_fusion
  140.6 0.6 add_convert_fusion.1
  141.3 2.1 pad_maximum_fusion
  143.4 1.0 copy-done.6
  144.4 0.3 fusion.17
  144.7 1.3 convolution_add_fusion.3
  146.0 19.6 %all-gather.9.cloned.1.call-done = f32[4096,64]{0,1:T(8,128)} async-done(((f32[512,64]{0,1:T(8,128)}), f32[4096,64]{0,1:T(8,128)}) %all-gather.9.cloned.1.call-update) | async-done | bytes 1048592 | tf_op jit(solution)/shard_map/all_gather | solution.py:90
  165.6 1.8 copy.24
  167.4 0.3 bitcast_reduce_fusion
  167.7 0.3 multiply_convert_fusion
  168.0 1.1 convolution_convert_fusion.3
  169.1 15.3 %all-to-all-start.3 = ((bf16[64,2,128]{2,1,0:T(2,128)(2,1)}), bf16[64,2,128]{2,1,0:T(2,128)(2,1)S(1)}, u32[]{:S(2)}, u32[]{:S(2)}) async-start(bf16[64,2,128]{2,1,0:T(2,128)(2,1)} %bitcast.20), calls=%async_computation.4 | async-start | bytes 65536 | tf_op jit(solution)/shard_map/all_to_all | solution.py:47
  184.5 28.5 %reduce-scatter.2.cloned.1.call-done = bf16[128,1792]{1,0:T(8,128)(2,1)} async-done(((bf16[1024,1792]{1,0:T(8,128)(2,1)}), bf16[128,1792]{1,0:T(8,128)(2,1)}) %reduce-scatter.2.cloned.1.call-update) | async-done | bytes 458768 | tf_op jit(solution)/shard_map/reduce_scatter | solution.py:82
  212.9 2.0 reshape.65
  214.9 15.0 %all-to-all-start.2 = ((bf16[64,2,1792]{2,1,0:T(2,128)(2,1)}), bf16[64,2,1792]{2,1,0:T(2,128)(2,1)S(1)}, u32[]{:S(2)}, u32[]{:S(2)}) async-start(bf16[64,2,1792]{2,1,0:T(2,128)(2,1)} %reshape.65), calls=%async_computation.3 | async-start | bytes 917504 | tf_op jit(solution)/shard_map/all_to_all | solution.py:47
  229.9 0.7 fusion.43
  230.6 28.2 %all-to-all-done.2 = bf16[64,2,1792]{2,1,0:T(2,128)(2,1)S(1)} async-done(((bf16[64,2,1792]{2,1,0:T(2,128)(2,1)}), bf16[64,2,1792]{2,1,0:T(2,128)(2,1)S(1)}, u32[]{:S(2)}, u32[]{:S(2)}) %all-to-all-start.2) | async-done | bytes 458784 | tf_op jit(solution)/shard_map/all_to_all | solution.py:47
  258.8 0.2 reshape.66
  259.0 0.9 convolution_convert_fusion.2
  (27 shorter events, 0.2 us)
Async XLA Ops:
  7.2 160.8 %copy-start = (bf16[1,128,4096]{2,1,0:T(8,128)(2,1)S(1)}, bf16[1,128,4096]{2,1,0:T(8,128)(2,1)}, u32[]{:S(2)}) copy-start(bf16[1,128,4096]{2,1,0:T(8,128)(2,1)} %param.21) | copy-start | bytes 3145732
  7.2 85.2 %all-gather.5.cloned.1.call-start = ((), (), s32[]{:S(2)}) async-start(), calls=%async_computation.5 | async-start | bytes 4128768 | tf_op jit(solution)/shard_map/all_gather | solution.py:53
  9.1 47.8 %copy-start.9 = (bf16[64,1792]{1,0:T(8,128)(2,1)S(1)}, bf16[64,1792]{1,0:T(8,128)(2,1)}, u32[]{:S(2)}) copy-start(bf16[64,1792]{1,0:T(8,128)(2,1)} %param.11) | copy-start | bytes 688132
  56.8 70.5 %all-gather.7.cloned.1.call-start = ((), (), s32[]{:S(2)}) async-start(), calls=%async_computation.6 | async-start | bytes 4128768 | tf_op jit(solution)/shard_map/all_gather | solution.py:53
  92.3 73.2 %all-gather.9.cloned.1.call-start = ((), (), s32[]{:S(2)}) async-start(), calls=%async_computation.8 | async-start | bytes 1179648 | tf_op jit(solution)/shard_map/all_gather | solution.py:90
  127.4 2.4 copy-start.1
  129.8 1.2 copy-start.3
  132.2 1.4 copy-start.10
  132.9 0.7 copy-start.7
  134.5 78.4 %reduce-scatter.2.cloned.1.call-start = ((), (), s32[]{:S(2)}) async-start(), calls=%async_computation.7 | async-start | bytes 4128768 | tf_op jit(solution)/shard_map/reduce_scatter | solution.py:82
  134.6 1.8 copy-start.5
  134.6 1.8 copy-start.8
  136.4 1.8 copy-start.2
  138.8 1.2 copy-start.4
  143.4 1.0 copy-start.6
  169.1 45.8 %all-to-all-start.3 = ((bf16[64,2,128]{2,1,0:T(2,128)(2,1)}), bf16[64,2,128]{2,1,0:T(2,128)(2,1)S(1)}, u32[]{:S(2)}, u32[]{:S(2)}) async-start(bf16[64,2,128]{2,1,0:T(2,128)(2,1)} %bitcast.20), calls=%async_computation.4 | async-start | bytes 65536 | tf_op jit(solution)/shard_map/all_to_all | solution.py:47
  214.9 43.9 %all-to-all-start.2 = ((bf16[64,2,1792]{2,1,0:T(2,128)(2,1)}), bf16[64,2,1792]{2,1,0:T(2,128)(2,1)S(1)}, u32[]{:S(2)}, u32[]{:S(2)}) async-start(bf16[64,2,1792]{2,1,0:T(2,128)(2,1)} %reshape.65), calls=%async_computation.3 | async-start | bytes 917504 | tf_op jit(solution)/shard_map/all_to_all | solution.py:47
Sparse Core Ops, SparseCore 0:
  57.0 30.6 all-gather.4
  92.5 34.8 all-gather.6
  134.6 30.9 all-gather.8
  168.3 44.6 reduce-scatter.1
